TPU v7x, 128 devices: a whole 4x4x4 slice. The times are simulated.
128 devices in a mesh: tm: 32 (over x, y, z_hi), tensor: 4 (over z_lo, core).
Axes of the slice: x: 4, y: 4, z: 4 (z_hi: 2, z_lo: 2; z = z_hi * 2 + z_lo), core: 2. Of those that a mesh axis runs over, the one named last changes fastest.
Arguments:
- frames: bfloat16 [16384, 1408], P('tm'), may hold values from -6 to 6
- gain_attn: float32 [1408], replicated, may hold values from 0.25 to 1.75
- w_qkv: bfloat16 [1408, 3, 1408], P('tm', None, 'tensor')
- w_out: bfloat16 [1408, 1408], P('tensor', 'tm'), may hold values from -0.625 to 0.625
- gain_mlp: float32 [1408], replicated, may hold values from 0.25 to 1.75
- w_up: bfloat16 [1408, 6144], P('tm', 'tensor'), may hold values from -0.15625 to 0.15625
- w_down: bfloat16 [6144, 1408], P('tensor', 'tm'), may hold values from -0.078125 to 0.078125
- w_proj: bfloat16 [1408, 4096], P('tm', 'tensor'), may hold values from -0.15625 to 0.15625
- windows: int32 [256, 8], P('tm'), may hold values from 0 to 255, as said below
- pool_map: int32 [16384], P('tm'), may hold values from 0 to 15, as said below
- owners: int32 [4096, 1], P('tm'), may hold values from 0 to 31; in each aligned block of 128 rows (0 to 127, 128 to 255, ...) at most 8 rows name the same one
Outputs:
- received: bfloat16 [32, 256, 4096], P('tm', None, 'tensor')
Inputs may be any that keep to these rules, and one draw needn't show every extreme that they name: `windows`: row b lists 8 different blocks, each in the frame of block b or in the frame just before or just after it; frame f holds blocks 256 / 64 f onward. `pool_map`: in each aligned block of 64 patches every slot value is named by exactly 4 patches. `owners`: among the 128 rows of one index of tm no owner is named more than 8 times.
All inputs are finite; a program needn't handle non-finite values.
Results may differ from a plain program's by a relative error of at most 0.014.
The roundings to bfloat16 on the way count: a program that leaves them out, or rounds other values in their place, can miss the bound.
Values may be sent and summed in bfloat16 or wider, within the bound.
A program may use at most 64 MiB of HBM per device.

v0:
```python
import math
import jax
import jax.numpy as jnp
from jax import lax
from jax.sharding import PartitionSpec as P

D = 1408
HEADS = 16
PATCHES = 256
BLK = 64
WIN = 8
POOL = 4
eps = 1e-06


def with_halo(block, sides, width):
    for axis, dim in sides:
        count = lax.axis_size(axis)
        forward = [(i, i + 1) for i in range(count - 1)]
        backward = [(target, source) for source, target in forward]
        low = lax.ppermute(
            lax.slice_in_dim(block, block.shape[dim] - width, None, axis=dim), axis, forward
        )
        high = lax.ppermute(lax.slice_in_dim(block, 0, width, axis=dim), axis, backward)
        block = jnp.concatenate([low, block, high], axis=dim)
    return block


def layer_norm(values, scales):
    average = jnp.mean(values, axis=-1, keepdims=True)
    centred = values - average
    spread = jnp.mean(centred * centred, axis=-1, keepdims=True)
    return (centred * lax.rsqrt(spread + eps) * scales).astype(jnp.bfloat16)


def pool_rows(values, slot_map):
    block_count = values.shape[0] // BLK
    slot_ids = jnp.arange(BLK // POOL, dtype=jnp.int32)
    chooser = (slot_map.reshape(block_count, 1, BLK) == slot_ids[None, :, None]).astype(jnp.float32)
    summed = jnp.einsum(
        "bsp,bpd->bsd",
        chooser,
        values.reshape(block_count, BLK, values.shape[1]),
        precision=lax.Precision.HIGHEST,
    )
    return (
        (summed * (1.0 / POOL))
        .reshape(block_count * (BLK // POOL), values.shape[1])
        .astype(jnp.bfloat16)
    )


def tensor_total(term):
    return lax.psum(term.astype(jnp.bfloat16), "tensor").astype(jnp.float32)


def body(
    frames, gain_attn, w_qkv, w_out, gain_mlp, w_up, w_down, w_proj, windows, pool_map, owners
):
    row_count = frames.shape[0]
    query_blocks = row_count // BLK
    head_dim = D // HEADS
    full_qkv, full_out, full_up, full_down, full_proj = (
        lax.all_gather(w_qkv, "tm", axis=0, tiled=True),
        lax.all_gather(w_out, "tm", axis=1, tiled=True),
        lax.all_gather(w_up, "tm", axis=0, tiled=True),
        lax.all_gather(w_down, "tm", axis=1, tiled=True),
        lax.all_gather(w_proj, "tm", axis=0, tiled=True),
    )
    local_width = full_qkv.shape[2]
    heads_here = local_width // head_dim
    normed = layer_norm(frames.astype(jnp.float32), gain_attn)
    projected_qkv = jnp.dot(
        normed, full_qkv.reshape(D, 3 * local_width), preferred_element_type=jnp.float32
    ).astype(jnp.bfloat16)
    projected_qkv = projected_qkv.reshape(row_count, 3, local_width)
    keyvals = with_halo(projected_qkv[:, 1:, :], (("tm", 0),), PATCHES)
    per_frame = PATCHES // BLK
    kv_blocks = keyvals.reshape(query_blocks + 2 * per_frame, BLK, 2, heads_here, head_dim)
    local_ids = windows - (lax.axis_index("tm") * query_blocks - per_frame)
    group_size = math.gcd(query_blocks, 8)
    queries = projected_qkv[:, 0, :].reshape(
        query_blocks // group_size, group_size, BLK, heads_here, head_dim
    )
    score_scale = head_dim ** (-0.5)

    def attend_group(packed):
        query_group, id_group = packed
        picked = kv_blocks[id_group].reshape(group_size, WIN * BLK, 2, heads_here, head_dim)
        scores = (
            jnp.einsum(
                "gqhd,gkhd->ghqk", query_group, picked[:, :, 0], preferred_element_type=jnp.float32
            )
            * score_scale
        )
        row_top = jnp.max(scores, axis=-1, keepdims=True)
        expw = jnp.exp(scores - row_top)
        attn_probs = (expw / jnp.sum(expw, axis=-1, keepdims=True)).astype(jnp.bfloat16)
        return jnp.einsum(
            "ghqk,gkhd->gqhd", attn_probs, picked[:, :, 1], preferred_element_type=jnp.float32
        ).astype(jnp.bfloat16)

    attended = lax.map(
        attend_group, (queries, local_ids.reshape(query_blocks // group_size, group_size, WIN))
    ).reshape(row_count, local_width)
    mixed_term = jnp.dot(attended, full_out, preferred_element_type=jnp.float32)
    stream = frames.astype(jnp.float32) + tensor_total(mixed_term)
    hidden = layer_norm(stream, gain_mlp)
    activation = jax.nn.gelu(
        jnp.dot(hidden, full_up, preferred_element_type=jnp.float32), approximate=False
    ).astype(jnp.bfloat16)
    stream = stream + tensor_total(
        jnp.dot(activation, full_down, preferred_element_type=jnp.float32)
    )
    pooled = pool_rows(stream, pool_map)
    proj_rows = jnp.dot(pooled, full_proj, preferred_element_type=jnp.float32).astype(jnp.bfloat16)
    pooled_count = proj_rows.shape[0]
    owner_count = lax.axis_size("tm")
    capacity = 2 * pooled_count // owner_count
    owner_ids = owners[:, 0]
    owner_hits = (owner_ids[:, None] == jnp.arange(owner_count, dtype=jnp.int32)[None, :]).astype(
        jnp.int32
    )
    slot_rank = jnp.sum((jnp.cumsum(owner_hits, axis=0) - 1) * owner_hits, axis=1)
    slot_dest = owner_ids * capacity + slot_rank
    placement = (
        jnp.arange(owner_count * capacity, dtype=jnp.int32)[:, None] == slot_dest[None, :]
    ).astype(jnp.bfloat16)
    outbox = jnp.dot(placement, proj_rows, preferred_element_type=jnp.float32).astype(jnp.bfloat16)
    outbox = outbox.reshape(owner_count, capacity, proj_rows.shape[1])
    received = lax.all_to_all(outbox, "tm", split_axis=0, concat_axis=0, tiled=True)
    return received.reshape(1, owner_count * capacity, proj_rows.shape[1])


def solution(mesh):
    placed = (
        P("tm", None),
        P(),
        P("tm", None, "tensor"),
        P("tensor", "tm"),
        P(),
        P("tm", "tensor"),
        P("tensor", "tm"),
        P("tm", "tensor"),
        P("tm", None),
        P("tm"),
        P("tm", None),
    )
    return jax.shard_map(
        body, mesh=mesh, in_specs=placed, out_specs=P("tm", None, "tensor"), check_vma=False
    )
```

profile of v0, /device:TPU:0, one launch (start us, length us, event | category | flops | bytes accessed | tf_op | source)
XLA Modules:
  0.0 647.8 jit_solution(6431842312539559043)
XLA Ops:
  6.5 1.6 copy.23
  9.0 1.6 convert_reduce_fusion
  10.6 1.9 fusion.16
  12.5 83.1 %all-gather.9.cloned.1.call-done = bf16[1408,3,352]{2,1,0:T(4,128)(2,1)} async-done(((bf16[44,3,352]{2,1,0:T(4,128)(2,1)}), bf16[1408,3,352]{2,1,0:T(4,128)(2,1)}) %all-gather.9.cloned.1.call-update) | async-done | bytes 2973712 | tf_op jit(solution)/shard_map/all_gather | solution.py:64
  95.6 7.7 %copy.24 = bf16[1408,3,352]{0,2,1:T(8,128)(2,1)} copy(bf16[1408,3,352]{2,1,0:T(4,128)(2,1)} %all-gather.9.cloned.1.call-done) | data formatting | bytes 5947392 | tf_op jit(solution)/shard_map/all_gather | solution.py:64
  103.3 3.9 convolution_convert_fusion.2
  108.4 2.3 collective-permute-start
  113.0 102.0 %all-gather = bf16[32,44,352]{2,1,0:T(8,128)(2,1)S(1)} all-gather(bf16[1,44,352]{2,1,0:T(8,128)(2,1)S(1)} %bitcast.53), channel_id=1, replica_groups=mesh['tm'=32,'tensor'=4] {'tm'}, dimensions={0}, use_global_device_ids=true | all-gather | bytes 1022208 | tf_op jit(solution)/shard_map/all_gather | solution.py:65
  222.2 2.3 reshape.72
  224.5 2.1 copy.28
  226.6 5.5 gather_fusion
  232.2 9.4 %copy.29 = bf16[64,64,2,4,88]{4,1,0,3,2:T(8,128)(2,1)} copy(bf16[64,64,2,4,88]{4,1,3,2,0:T(8,128)(2,1)} %gather_fusion) | data formatting | bytes 11534336 | tf_op jit(solution)/shard_map/while/body/eval_jaxpr/gather | solution.py:89
  241.5 5.9 fusion.110
  247.4 6.2 copy.40
  253.6 2.6 fusion.19
  256.2 2.8 fusion.112
  259.0 6.1 copy.38
  265.1 4.4 fusion.72
  270.3 2.0 convolution_convert_fusion.1
  274.6 41.4 %all-reduce.3.cloned.1.call-done = bf16[512,1408]{1,0:T(8,128)(2,1)} async-done(((bf16[512,1408]{1,0:T(8,128)(2,1)}), bf16[512,1408]{1,0:T(8,128)(2,1)}) %all-reduce.3.cloned.1.call-update) | async-done | bytes 1441808 | tf_op jit(solution)/shard_map/psum | solution.py:54
  315.9 1.9 fusion.24
  318.5 86.1 %all-gather.11.cloned.1.call-done = bf16[32,44,1536]{2,1,0:T(8,128)(2,1)} async-done(((bf16[1,44,1536]{2,1,0:T(8,128)(2,1)}), bf16[32,44,1536]{2,1,0:T(8,128)(2,1)}) %all-gather.11.cloned.1.call-update) | async-done | bytes 4325392 | tf_op jit(solution)/shard_map/all_gather | solution.py:66
  404.6 7.0 %reshape.92 = bf16[1408,1536]{1,0:T(8,128)(2,1)} reshape(bf16[32,44,1536]{2,1,0:T(8,128)(2,1)} %all-gather.11.cloned.1.call-done) | data formatting | bytes 8650752
  411.7 77.3 %all-gather.13.cloned.1.call-done = bf16[32,44,1536]{2,1,0:T(8,128)(2,1)} async-done(((bf16[1,44,1536]{2,1,0:T(8,128)(2,1)}), bf16[32,44,1536]{2,1,0:T(8,128)(2,1)}) %all-gather.13.cloned.1.call-update) | async-done | bytes 4325392 | tf_op jit(solution)/shard_map/all_gather | solution.py:67
  488.9 7.0 %reshape.94 = bf16[1408,1536]{1,0:T(8,128)(2,1)} reshape(bf16[32,44,1536]{2,1,0:T(8,128)(2,1)} %all-gather.13.cloned.1.call-done) | data formatting | bytes 8650752
  496.0 15.1 %convolution_convert_fusion = bf16[512,1408]{1,0:T(8,128)(2,1)} fusion(bf16[1408,1536]{1,0:T(8,128)(2,1)} %reshape.94, bf16[1408,1536]{1,0:T(8,128)(2,1)} %reshape.92, bf16[512,1408]{1,0:T(8,128)(2,1)S(1)} %copy-done.1, bf16[512,1408]{1,0:T(8,128)(2,1)S(1)} %copy-done, f32[1408]{0:T(1024)S(1)} %copy-done.9, f32[512]{0:T(512)S(1)} %add_rsqrt_fusion, ...), kind=kOutput, calls=%fused_computation.30 | convolution fusion | flops 4486070272 | bytes 12985856 | tf_op jit(solution)/shard_map/dot_general | solution.py:113
  511.6 54.0 %all-gather.15.cloned.1.call-done = bf16[32,44,1024]{2,1,0:T(8,128)(2,1)} async-done(((bf16[1,44,1024]{2,1,0:T(8,128)(2,1)}), bf16[32,44,1024]{2,1,0:T(8,128)(2,1)}) %all-gather.15.cloned.1.call-update) | async-done | bytes 2883600 | tf_op jit(solution)/shard_map/all_gather | solution.py:68
  565.6 5.2 reshape.96
  570.8 40.6 %all-reduce.5.cloned.1.call-done = bf16[512,1408]{1,0:T(8,128)(2,1)} async-done(((bf16[512,1408]{1,0:T(8,128)(2,1)}), bf16[512,1408]{1,0:T(8,128)(2,1)}) %all-reduce.5.cloned.1.call-update) | async-done | bytes 1441808 | tf_op jit(solution)/shard_map/psum | solution.py:54
  611.5 1.8 convert_add_fusion.1
  614.4 2.6 fusion.71
  617.0 23.1 %all_to_all.5 = bf16[32,8,1024]{2,1,0:T(8,128)(2,1)S(1)} all-to-all(bf16[32,8,1024]{2,1,0:T(8,128)(2,1)S(1)} %fusion.71), channel_id=1, replica_groups=mesh['tm'=32,'tensor'=4] {'tm'}, dimensions={0} | all-to-all | bytes 1048576 | tf_op jit(solution)/shard_map/all_to_all | solution.py:131
  (61 shorter events, 17.5 us)
Async XLA Ops:
  6.5 89.1 %all-gather.9.cloned.1.call-start = ((), (), s32[]{:S(2)}) async-start(), calls=%async_computation.1 | async-start | bytes 4460544 | tf_op jit(solution)/shard_map/all_gather | solution.py:64
  8.2 307.8 %all-reduce.3.cloned.1.call-start = ((), (), s32[]{:S(2)}) async-start(), calls=%async_computation.2 | async-start | bytes 2883584 | tf_op jit(solution)/shard_map/psum | solution.py:54
  12.5 90.8 %copy-start = (bf16[512,1408]{1,0:T(8,128)(2,1)S(1)}, bf16[512,1408]{1,0:T(8,128)(2,1)}, u32[]{:S(2)}) copy-start(bf16[512,1408]{1,0:T(8,128)(2,1)} %param.11) | copy-start | bytes 4325380
  12.5 90.8 %copy-start.8 = (f32[1408]{0:T(1024)S(1)}, f32[1408]{0:T(1024)}, u32[]{:S(2)}) copy-start(f32[1408]{0:T(1024)} %param.12) | copy-start | bytes 16900
  103.3 9.7 %copy-start.5 = (bf16[352,44]{0,1:T(8,128)(2,1)S(1)}, bf16[352,44]{0,1:T(8,128)(2,1)}, u32[]{:S(2)}) copy-start(bf16[352,44]{0,1:T(8,128)(2,1)} %param.14) | copy-start | bytes 92932
  107.2 1.0 copy-start.4
  108.4 112.3 %collective-permute-start = (bf16[256,2,352]{2,0,1:T(8,128)(2,1)S(1)}, bf16[256,2,352]{2,0,1:T(8,128)(2,1)S(1)}, u32[]{:S(2)}, u32[]{:S(2)}) collective-permute-start(bf16[256,2,352]{2,0,1:T(8,128)(2,1)S(1)} %copy.35), channel_id=1, source_target_pairs={{0,4},{4,8},{8,12},{12,16},{16,20},{20,24},{24,28},{28,32},{32,36}... | collective-permute-start | bytes 1081352 | tf_op jit(solution)/shard_map/ppermute | solution.py:21
  111.7 109.1 %collective-permute-start.1 = (bf16[256,2,352]{2,0,1:T(8,128)(2,1)}, bf16[256,2,352]{2,0,1:T(8,128)(2,1)}, u32[]{:S(2)}, u32[]{:S(2)}) collective-permute-start(bf16[256,2,352]{2,0,1:T(8,128)(2,1)} %copy.37), channel_id=1, source_target_pairs={{4,0},{8,4},{12,8},{16,12},{20,16},{24,20},{28,24},{32,28},{36,32}... | collective-permute-start | bytes 1081352 | tf_op jit(solution)/shard_map/ppermute | solution.py:24
  247.4 6.2 copy-start.2
  265.1 5.2 copy-start.3
  272.4 132.2 %all-gather.11.cloned.1.call-start = ((), (), s32[]{:S(2)}) async-start(), calls=%async_computation.4 | async-start | bytes 4866048 | tf_op jit(solution)/shard_map/all_gather | solution.py:66
  273.1 215.8 %all-gather.13.cloned.1.call-start = ((), (), s32[]{:S(2)}) async-start(), calls=%async_computation.5 | async-start | bytes 4866048 | tf_op jit(solution)/shard_map/all_gather | solution.py:67
  273.7 291.9 %all-gather.15.cloned.1.call-start = ((), (), s32[]{:S(2)}) async-start(), calls=%async_computation.6 | async-start | bytes 3244032 | tf_op jit(solution)/shard_map/all_gather | solution.py:68
  274.3 337.2 %all-reduce.5.cloned.1.call-start = ((), (), s32[]{:S(2)}) async-start(), calls=%async_computation.3 | async-start | bytes 2883584 | tf_op jit(solution)/shard_map/psum | solution.py:54
  315.9 1.9 copy-start.1
  411.7 84.3 %copy-start.9 = (f32[1408]{0:T(1024)S(1)}, f32[1408]{0:T(1024)}, u32[]{:S(2)}) copy-start(f32[1408]{0:T(1024)} %param.15) | copy-start | bytes 16900
  496.0 15.1 %copy-start.7 = (s32[512]{0:T(512)S(1)}, s32[512]{0:T(512)}, u32[]{:S(2)}) copy-start(s32[512]{0:T(512)} %param.20) | copy-start | bytes 6148
  496.0 15.2 %copy-start.6 = (s32[128,1]{0,1:T(1,128)S(1)}, s32[128,1]{0,1:T(1,128)}, u32[]{:S(2)}) copy-start(s32[128,1]{0,1:T(1,128)} %param.21) | copy-start | bytes 1540
Sparse Core Ops, SparseCore 0:
  10.3 85.2 all-gather.8
  272.5 43.3 all-reduce.2
  318.9 85.6 all-gather.10
  407.4 81.4 all-gather.12
  491.7 73.8 all-gather.14
  568.0 43.4 all-reduce.4
where the time goes:
time: 649 us; the launch traced here: 648 us
  waiting for transfers between devices  384 us (59%)
  blocking collectives  125 us (19%)
  local copies, waits for them, and re-layouts  75.8 us (12%)
  matrix products  31.7 us (5%)
  between operations  13.7 us (2%)
  other arithmetic  13.3 us (2%)
    all_gather x1, blocking collectives, body(): lax.all_gather(w_out, 'tm', axis=1, tiled=True)  102 us
    all_gather x1, waiting for transfers between devices, body(): lax.all_gather(w_up, 'tm', axis=0, tiled=True)  86.1 us
    all_gather x1, waiting for transfers between devices, body(): lax.all_gather(w_qkv, 'tm', axis=0, tiled=True)  83.1 us
    psum x2, waiting for transfers between devices, tensor_total(): return lax.psum(term.astype(jnp.bfloat16), 'tensor').astype(jnp.float32)  82 us
    all_gather x1, waiting for transfers between devices, body(): lax.all_gather(w_down, 'tm', axis=1, tiled=True)  77.3 us
    all_gather x1, waiting for transfers between devices, body(): lax.all_gather(w_proj, 'tm', axis=0, tiled=True)  54 us
    unnamed x31, local copies, waits for them, and re-layouts  38.5 us
    all_to_all x1, blocking collectives, body(): lax.all_to_all(outbox, 'tm', split_axis=0, concat_axis=0, tiled=True)  23.1 us
  transfers between devices with their start and end apart: 8, of which 6 were waited for; matrix products, arithmetic and copies ran while one was open for 7% of the time, Pallas kernels for 0%

commit v1 on v0

--- a/solution.py
+++ b/solution.py
@@ -51,7 +51,11 @@
 
 
 def tensor_total(term):
-    return lax.psum(term.astype(jnp.bfloat16), "tensor").astype(jnp.float32)
+
+    def put_the_corner(t0, net_axis):
+        return jnp.sum(lax.all_gather(t0, net_axis), axis=0)
+
+    return put_the_corner(term.astype(jnp.bfloat16), "tensor").astype(jnp.float32)
 
 
 def body(

time: 649 us -> 517 us (0.80)
  waiting for transfers between devices: 384 us -> 240 us
  other arithmetic: 13.3 us -> 23 us
    all_gather x0 -> x2, waiting for transfers between devices: none -> 95 us  [put_the_corner(): return jnp.sum(lax.all_gather(t0, net_axis), axis=0)]
    all_gather x1, waiting for transfers between devices: 86.1 us -> 0.02 us  [body(): lax.all_gather(w_up, 'tm', axis=0, tiled=True)]
    psum x2 -> x0, waiting for transfers between devices: 82 us -> none  [tensor_total(): return lax.psum(term.astype(jnp.bfloat16), 'tensor').astype(jnp.float32)]
    all_gather x1, waiting for transfers between devices: 77.3 us -> 0.01 us  [body(): lax.all_gather(w_down, 'tm', axis=1, tiled=True)]
    reduce_sum x0 -> x2, other arithmetic: none -> 9.39 us  [put_the_corner(): return jnp.sum(lax.all_gather(t0, net_axis), axis=0)]
  transfers between devices with their start and end apart: 8 -> 8, of which waited for: 6 -> 4; matrix products, arithmetic and copies ran while one was open for 7% -> 22% of each run, Pallas kernels for 0% -> 0%
where the time goes in v1:
time: 517 us; the launch traced here: 515 us
  waiting for transfers between devices  240 us (46%)
  blocking collectives  129 us (25%)
  local copies, waits for them, and re-layouts  76.8 us (15%)
  matrix products  28.7 us (6%)
  other arithmetic  23 us (4%)
  between operations  13.7 us (3%)
    all_gather x1, blocking collectives, body(): lax.all_gather(w_out, 'tm', axis=1, tiled=True)  105 us
    all_gather x2, waiting for transfers between devices, put_the_corner(): return jnp.sum(lax.all_gather(t0, net_axis), axis=0)  95 us
    all_gather x1, waiting for transfers between devices, body(): lax.all_gather(w_qkv, 'tm', axis=0, tiled=True)  82.8 us
    all_gather x1, waiting for transfers between devices, body(): lax.all_gather(w_proj, 'tm', axis=0, tiled=True)  60.4 us
    unnamed x31, local copies, waits for them, and re-layouts  38.9 us
    all_to_all x1, blocking collectives, body(): lax.all_to_all(outbox, 'tm', split_axis=0, concat_axis=0, tiled=True)  23.9 us
    dot_general x1, matrix products, body(): jnp.dot(activation, full_down, preferred_element_type=jnp.float32)  15.2 us
    gather x2, local copies, waits for them, and re-layouts, attend_group(): kv_blocks[id_group].reshape(group_size, WIN * BLK, 2, heads_here, head_dim)  15 us
  transfers between devices with their start and end apart: 8, of which 4 were waited for; matrix products, arithmetic and copies ran while one was open for 22% of the time, Pallas kernels for 0%

profile of v1, /device:TPU:0, one launch (start us, length us, event | category | flops | bytes accessed | tf_op | source)
XLA Modules:
  0.0 514.9 jit_solution(17916478248998559553)
XLA Ops:
  6.5 1.7 copy.23
  10.6 1.6 convert_reduce_fusion
  12.8 82.8 %all-gather.13.cloned.1.call-done = bf16[1408,3,352]{2,1,0:T(4,128)(2,1)} async-done(((bf16[44,3,352]{2,1,0:T(4,128)(2,1)}), bf16[1408,3,352]{2,1,0:T(4,128)(2,1)}) %all-gather.13.cloned.1.call-update) | async-done | bytes 2973712 | tf_op jit(solution)/shard_map/all_gather | solution.py:68
  95.6 7.7 %copy.24 = bf16[1408,3,352]{0,2,1:T(8,128)(2,1)} copy(bf16[1408,3,352]{2,1,0:T(4,128)(2,1)} %all-gather.13.cloned.1.call-done) | data formatting | bytes 5947392 | tf_op jit(solution)/shard_map/all_gather | solution.py:68
  103.3 3.9 convolution_convert_fusion.2
  108.4 2.3 collective-permute-start
  111.7 1.3 collective-permute-start.1
  113.0 104.7 %all-gather.2 = bf16[32,44,352]{2,1,0:T(8,128)(2,1)S(1)} all-gather(bf16[1,44,352]{2,1,0:T(8,128)(2,1)S(1)} %bitcast.57), channel_id=1, replica_groups=mesh['tm'=32,'tensor'=4] {'tm'}, dimensions={0}, use_global_device_ids=true | all-gather | bytes 1022208 | tf_op jit(solution)/shard_map/all_gather | solution.py:69
  223.5 1.4 pad_maximum_fusion
  224.9 2.3 reshape.72
  227.2 2.2 copy.28
  229.3 5.6 %gather_fusion = bf16[64,64,2,4,88]{4,1,3,2,0:T(8,128)(2,1)} fusion(bf16[16,64,2,4,88]{4,1,3,2,0:T(8,128)(2,1)S(1)} %copy.28, s32[1024]{0:T(1024)S(1)} %pad_clamp_fusion), kind=kCustom, calls=%fused_computation | custom fusion | bytes 11534592 | tf_op jit(solution)/shard_map/while/body/eval_jaxpr/gather | solution.py:93
  234.9 9.4 %copy.29 = bf16[64,64,2,4,88]{4,1,0,3,2:T(8,128)(2,1)} copy(bf16[64,64,2,4,88]{4,1,3,2,0:T(8,128)(2,1)} %gather_fusion) | data formatting | bytes 11534336 | tf_op jit(solution)/shard_map/while/body/eval_jaxpr/gather | solution.py:93
  244.3 6.4 %fusion.110 = (bf16[8,512,1,4,88]{4,1,0,3,2:T(8,128)(2,1)}, bf16[8,512,1,4,88]{4,1,0,3,2:T(8,128)(2,1)}) fusion(bf16[8,512,2,4,88]{4,1,0,3,2:T(8,128)(2,1)} %bitcast.44), kind=kLoop, calls=%fused_computation.136 | loop fusion | bytes 11534336 | tf_op jit(solution)/shard_map/while/body/eval_jaxpr/slice | solution.py:104
  250.7 6.1 %copy.40 = bf16[8,512,1,4,88]{1,4,3,0,2:T(8,128)(2,1)} copy(bf16[8,512,1,4,88]{4,1,0,3,2:T(8,128)(2,1)} %get-tuple-element.14) | data formatting | bytes 5767168
  256.8 6.2 %copy.38 = bf16[8,512,1,4,88]{1,4,3,0,2:T(8,128)(2,1)} copy(bf16[8,512,1,4,88]{4,1,0,3,2:T(8,128)(2,1)} %get-tuple-element.13) | data formatting | bytes 5767168
  263.0 2.6 fusion.19
  265.6 6.0 %fusion.112 = (f32[8,4,64]{2,1,0:T(4,128)S(1)}, f32[8,4,64,512]{3,2,1,0:T(8,128)S(1)}) fusion(f32[8,4,64,512]{3,2,1,0:T(8,128)S(1)} %fusion.19), kind=kOutput, calls=%fused_computation.138 | output fusion | flops 4194815 | bytes 8396800 | tf_op jit(solution)/shard_map/while/body/eval_jaxpr/sub | solution.py:101
  271.6 1.3 fusion.72
  273.6 2.0 convolution_convert_fusion.1
  276.3 7.0 %reshape.94 = bf16[1408,1536]{1,0:T(8,128)(2,1)} reshape(bf16[32,44,1536]{2,1,0:T(8,128)(2,1)} %all-gather.19.cloned.1.call-done) | data formatting | bytes 8650752
  283.4 7.4 %reshape.96 = bf16[1408,1536]{1,0:T(8,128)(2,1)} reshape(bf16[32,44,1536]{2,1,0:T(8,128)(2,1)} %all-gather.21.cloned.1.call-done) | data formatting | bytes 8650752
  290.8 43.3 %all-gather.15.cloned.1.call-done = bf16[2048,1408]{1,0:T(8,128)(2,1)} async-done(((bf16[512,1408]{1,0:T(8,128)(2,1)}), bf16[2048,1408]{1,0:T(8,128)(2,1)}) %all-gather.15.cloned.1.call-update) | async-done | bytes 5767184 | tf_op jit(solution)/shard_map/all_gather | solution.py:56
  334.1 4.4 reduce_sum.83
  339.6 15.2 %convolution_convert_fusion = bf16[512,1408]{1,0:T(8,128)(2,1)} fusion(bf16[1408,1536]{1,0:T(8,128)(2,1)} %reshape.96, bf16[1408,1536]{1,0:T(8,128)(2,1)} %reshape.94, bf16[512,1408]{1,0:T(8,128)(2,1)S(1)} %reduce_sum.83, bf16[512,1408]{1,0:T(8,128)(2,1)S(1)} %copy-done, f32[1408]{0:T(1024)S(1)} %copy-done.9, f32[512]{0:T(512)S(1)} %add_rsqrt_fusion, ...), kind=kOutput, calls=%fused_computation.30 | convolution fusion | flops 4486070272 | bytes 12985856 | tf_op jit(solution)/shard_map/dot_general | solution.py:117
  355.4 60.4 %all-gather.23.cloned.1.call-done = bf16[32,44,1024]{2,1,0:T(8,128)(2,1)} async-done(((bf16[1,44,1024]{2,1,0:T(8,128)(2,1)}), bf16[32,44,1024]{2,1,0:T(8,128)(2,1)}) %all-gather.23.cloned.1.call-update) | async-done | bytes 2883600 | tf_op jit(solution)/shard_map/all_gather | solution.py:72
  415.8 5.3 %reshape.98 = bf16[1408,1024]{1,0:T(8,128)(2,1)} reshape(bf16[32,44,1024]{2,1,0:T(8,128)(2,1)} %all-gather.23.cloned.1.call-done) | data formatting | bytes 5767168
  421.0 51.7 %all-gather.17.cloned.1.call-done = bf16[2048,1408]{1,0:T(8,128)(2,1)} async-done(((bf16[512,1408]{1,0:T(8,128)(2,1)}), bf16[2048,1408]{1,0:T(8,128)(2,1)}) %all-gather.17.cloned.1.call-update) | async-done | bytes 5767184 | tf_op jit(solution)/shard_map/all_gather | solution.py:56
  472.8 5.0 reduce_sum.86
  477.8 1.8 convert_add_fusion.1
  480.7 2.6 fusion.71
  483.3 23.9 %all_to_all.5 = bf16[32,8,1024]{2,1,0:T(8,128)(2,1)S(1)} all-to-all(bf16[32,8,1024]{2,1,0:T(8,128)(2,1)S(1)} %fusion.71), channel_id=1, replica_groups=mesh['tm'=32,'tensor'=4] {'tm'}, dimensions={0} | all-to-all | bytes 1048576 | tf_op jit(solution)/shard_map/all_to_all | solution.py:135
  (63 shorter events, 15.7 us)
Async XLA Ops:
  6.5 5.7 %copy-start = (bf16[512,1408]{1,0:T(8,128)(2,1)S(1)}, bf16[512,1408]{1,0:T(8,128)(2,1)}, u32[]{:S(2)}) copy-start(bf16[512,1408]{1,0:T(8,128)(2,1)} %param.11) | copy-start | bytes 4325380
  6.5 89.1 %all-gather.13.cloned.1.call-start = ((), (), s32[]{:S(2)}) async-start(), calls=%async_computation.1 | async-start | bytes 4460544 | tf_op jit(solution)/shard_map/all_gather | solution.py:68
  8.3 268.1 %all-gather.19.cloned.1.call-start = ((), (), s32[]{:S(2)}) async-start(), calls=%async_computation.4 | async-start | bytes 4866048 | tf_op jit(solution)/shard_map/all_gather | solution.py:70
  9.0 274.4 %all-gather.21.cloned.1.call-start = ((), (), s32[]{:S(2)}) async-start(), calls=%async_computation.5 | async-start | bytes 4866048 | tf_op jit(solution)/shard_map/all_gather | solution.py:71
  9.8 324.3 %all-gather.15.cloned.1.call-start = ((), (), s32[]{:S(2)}) async-start(), calls=%async_computation.2 | async-start | bytes 7208960 | tf_op jit(solution)/shard_map/all_gather | solution.py:56
  12.8 90.5 %copy-start.8 = (f32[1408]{0:T(1024)S(1)}, f32[1408]{0:T(1024)}, u32[]{:S(2)}) copy-start(f32[1408]{0:T(1024)} %param.12) | copy-start | bytes 16900
  103.3 9.7 %copy-start.5 = (bf16[352,44]{0,1:T(8,128)(2,1)S(1)}, bf16[352,44]{0,1:T(8,128)(2,1)}, u32[]{:S(2)}) copy-start(bf16[352,44]{0,1:T(8,128)(2,1)} %param.14) | copy-start | bytes 92932
  107.2 1.0 copy-start.3
  108.4 115.0 %collective-permute-start = (bf16[256,2,352]{2,0,1:T(8,128)(2,1)S(1)}, bf16[256,2,352]{2,0,1:T(8,128)(2,1)S(1)}, u32[]{:S(2)}, u32[]{:S(2)}) collective-permute-start(bf16[256,2,352]{2,0,1:T(8,128)(2,1)S(1)} %copy.35), channel_id=1, source_target_pairs={{0,4},{4,8},{8,12},{12,16},{16,20},{20,24},{24,28},{28,32},{32,36}... | collective-permute-start | bytes 1081352 | tf_op jit(solution)/shard_map/ppermute | solution.py:21
  111.7 111.8 %collective-permute-start.1 = (bf16[256,2,352]{2,0,1:T(8,128)(2,1)}, bf16[256,2,352]{2,0,1:T(8,128)(2,1)}, u32[]{:S(2)}, u32[]{:S(2)}) collective-permute-start(bf16[256,2,352]{2,0,1:T(8,128)(2,1)} %copy.37), channel_id=1, source_target_pairs={{4,0},{8,4},{12,8},{16,12},{20,16},{24,20},{28,24},{32,28},{36,32}... | collective-permute-start | bytes 1081352 | tf_op jit(solution)/shard_map/ppermute | solution.py:24
  256.8 6.2 %copy-start.1 = (bf16[8,64,4,88]{1,0,3,2:T(8,128)(2,1)S(1)}, bf16[8,64,4,88]{1,0,3,2:T(8,128)(2,1)}, u32[]{:S(2)}) copy-start(bf16[8,64,4,88]{1,0,3,2:T(8,128)(2,1)} %reshape.99) | copy-start | bytes 1081348
  265.6 6.0 %copy-start.4 = (bf16[8,512,1,4,88]{1,4,3,0,2:T(8,128)(2,1)S(1)}, bf16[8,512,1,4,88]{1,4,3,0,2:T(8,128)(2,1)}, u32[]{:S(2)}) copy-start(bf16[8,512,1,4,88]{1,4,3,0,2:T(8,128)(2,1)} %copy.38) | copy-start | bytes 8650756
  271.5 2.1 copy-start.2
  275.7 140.1 %all-gather.23.cloned.1.call-start = ((), (), s32[]{:S(2)}) async-start(), calls=%async_computation.6 | async-start | bytes 3244032 | tf_op jit(solution)/shard_map/all_gather | solution.py:72
  276.3 196.5 %all-gather.17.cloned.1.call-start = ((), (), s32[]{:S(2)}) async-start(), calls=%async_computation.3 | async-start | bytes 7208960 | tf_op jit(solution)/shard_map/all_gather | solution.py:56
  338.4 1.1 copy-start.9
  339.6 15.3 %copy-start.7 = (s32[512]{0:T(512)S(1)}, s32[512]{0:T(512)}, u32[]{:S(2)}) copy-start(s32[512]{0:T(512)} %param.20) | copy-start | bytes 6148
  339.6 15.3 %copy-start.6 = (s32[128,1]{0,1:T(1,128)S(1)}, s32[128,1]{0,1:T(1,128)}, u32[]{:S(2)}) copy-start(s32[128,1]{0,1:T(1,128)} %param.21) | copy-start | bytes 1540
Sparse Core Ops, SparseCore 0:
  10.3 85.2 all-gather.12
  98.5 94.0 all-gather.18
  195.6 81.3 all-gather.20
  278.5 55.5 all-gather.14
  336.9 78.8 all-gather.22
  417.3 55.4 all-gather.16
